TPU v7x, 32 devices: a whole 2x2x4 slice. The times are simulated.
32 devices in a mesh: wide: 8 (over z, x), narrow: 4 (over y, core).
Axes of the slice: x: 2, y: 2, z: 4, core: 2. Of those that a mesh axis runs over, the one named last changes fastest.
Arguments:
- states: bfloat16 [256, 262144], P('narrow', 'wide'), may hold values from -6 to 6
- obs_ens: bfloat16 [256, 32768], P('narrow', 'wide'), may hold values from -6 to 6
- obs_value: float32 [32768], P('wide'), may hold values from -6 to 6
- obs_prec: float32 [32768], P('wide'), may hold values from 0.1 to 1
- obs_pick: int32 [32, 1024], P('wide'), may hold values from 0 to 4607, as said below
- taper: float32 [32, 1024], P(('wide', 'narrow')), may hold values from 0.1 to 1
Outputs:
- analysis: bfloat16 [256, 262144], P('narrow', 'wide')
Inputs may be any that keep to these rules, and one draw needn't show every extreme that they name: `obs_pick`: within a region the 1024 rows are distinct.
All inputs are finite; a program needn't handle non-finite values.
Results may differ from a plain program's by a relative error of at most 0.0057.
Values may be sent and summed in bfloat16 or wider, within the bound.
No kernel may reach another device: no remote copies, remote signals or barrier semaphores. Data moves between devices by JAX's collectives and lax.ppermute only.
A program may use at most 64 MiB of HBM per device.

v0:
```python
import jax
import jax.numpy as jnp
from jax import lax
from jax.sharding import PartitionSpec as P

HALO = 256
ITERS = 6


def padded(array, sides, width):
    for axis, dim in sides:
        size, length = (lax.axis_size(axis), array.shape[dim])
        up = [(i, (i + 1) % size) for i in range(size)]
        down = [(j, i) for i, j in up]
        last = lax.slice_in_dim(array, length - width, length, axis=dim)
        leading = lax.slice_in_dim(array, 0, width, axis=dim)
        before = lax.ppermute(last, axis, up)
        after = lax.ppermute(leading, axis, down)
        array = jnp.concatenate([before, array, after], axis=dim)
    return array


def analyse(ensemble, observed, precision, taper_row, regional):
    members = ensemble.shape[0]
    obs_mean = jnp.mean(ensemble, axis=0)
    obs_pert = ensemble - obs_mean
    obs_weight = precision * taper_row
    scaled = (obs_pert * jnp.sqrt(obs_weight)).astype(jnp.bfloat16)
    identity = jnp.eye(members, dtype=jnp.float32)
    gram_sum = lax.dot_general(
        scaled, scaled, (((1,), (1,)), ((), ())), preferred_element_type=jnp.float32
    )
    precision_matrix = gram_sum + (members - 1.0) * identity
    forcing = jnp.dot(
        obs_pert,
        obs_weight * (observed - obs_mean),
        precision=lax.Precision.HIGHEST,
        preferred_element_type=jnp.float32,
    )
    norm_scale = jnp.sqrt(jnp.sum(precision_matrix * precision_matrix))
    current = precision_matrix / norm_scale
    root_iter = identity
    for iteration in range(ITERS):
        middle = 1.5 * identity - 0.5 * jnp.dot(
            root_iter, current, precision=lax.Precision.HIGHEST, preferred_element_type=jnp.float32
        )
        current = jnp.dot(
            current, middle, precision=lax.Precision.HIGHEST, preferred_element_type=jnp.float32
        )
        root_iter = jnp.dot(
            middle, root_iter, precision=lax.Precision.HIGHEST, preferred_element_type=jnp.float32
        )
    inv_root = root_iter / jnp.sqrt(norm_scale)
    inner = jnp.dot(
        inv_root, forcing, precision=lax.Precision.HIGHEST, preferred_element_type=jnp.float32
    )
    mean_weights = jnp.dot(
        inv_root, inner, precision=lax.Precision.HIGHEST, preferred_element_type=jnp.float32
    )
    transform = (jnp.sqrt(members - 1.0) * inv_root + mean_weights[:, None]).astype(jnp.bfloat16)
    state_mean = jnp.mean(regional.astype(jnp.float32), axis=0)
    state_pert = (regional.astype(jnp.float32) - state_mean).astype(jnp.bfloat16)
    mixed = lax.dot_general(
        transform, state_pert, (((0,), (0,)), ((), ())), preferred_element_type=jnp.float32
    )
    return (state_mean + mixed).astype(jnp.bfloat16)


def body(states, obs_ens, obs_value, obs_prec, obs_pick, taper):
    band_regions = lax.axis_size("narrow")
    position = lax.axis_index("narrow")
    members = obs_ens.shape[0] * band_regions
    extended = padded(obs_ens, (("wide", 1),), HALO)
    stat_pair = padded(jnp.stack([obs_value, obs_prec]), (("wide", 1),), HALO)
    own_rows = lax.dynamic_index_in_dim(obs_pick, position, 0, keepdims=False)
    chosen = jnp.take(extended, obs_pick.reshape(-1), axis=1).reshape(
        extended.shape[0], band_regions, -1
    )
    arrived = lax.all_to_all(chosen, "narrow", split_axis=1, concat_axis=0, tiled=True)
    picked = arrived.reshape(members, -1)
    stat_rows = jnp.take(stat_pair, own_rows, axis=1)
    regional = lax.all_to_all(states, "narrow", split_axis=1, concat_axis=0, tiled=True)
    result = analyse(picked.astype(jnp.float32), stat_rows[0], stat_rows[1], taper[0], regional)
    return lax.all_to_all(result, "narrow", split_axis=0, concat_axis=1, tiled=True)


def solution(mesh):
    return jax.shard_map(
        body,
        mesh=mesh,
        in_specs=(
            P("narrow", "wide"),
            P("narrow", "wide"),
            P("wide"),
            P("wide"),
            P("wide", None),
            P(("wide", "narrow"), None),
        ),
        out_specs=P("narrow", "wide"),
        check_vma=False,
    )
```

profile of v0, /device:TPU:0, one launch (start us, length us, event | category | flops | bytes accessed | tf_op | source)
XLA Modules:
  0.0 160.5 jit_solution(12780005530070920755)
XLA Ops:
  0.0 0.7 pad_maximum_fusion.3
  0.7 3.0 %collective-permute-start.2 = (f32[2,256]{1,0:T(2,128)S(1)}, f32[2,256]{1,0:T(2,128)S(1)}, u32[]{:S(2)}, u32[]{:S(2)}) collective-permute-start(f32[2,256]{1,0:T(2,128)S(1)} %get-tuple-element.11), channel_id=1, source_target_pairs={{0,4},{4,8},{8,12},{12,16},{16,20},{20,24},{24,28},{28,0},{1,5},{5... | collective-permute-start | bytes 6152 | tf_op jit(solution)/shard_map/ppermute | solution.py:17
  3.7 3.1 %collective-permute-start.3 = (f32[2,256]{1,0:T(2,128)S(1)}, f32[2,256]{1,0:T(2,128)S(1)}, u32[]{:S(2)}, u32[]{:S(2)}) collective-permute-start(f32[2,256]{1,0:T(2,128)S(1)} %get-tuple-element.12), channel_id=1, source_target_pairs={{4,0},{8,4},{12,8},{16,12},{20,16},{24,20},{28,24},{0,28},{5,1},{9... | collective-permute-start | bytes 6152 | tf_op jit(solution)/shard_map/ppermute | solution.py:18
  6.9 1.5 copy.24
  8.4 0.1 collective-permute-start
  8.5 4.7 %collective-permute-start.1 = (bf16[64,256]{0,1:T(8,128)(2,1)S(1)}, bf16[64,256]{0,1:T(8,128)(2,1)S(1)}, u32[]{:S(2)}, u32[]{:S(2)}) collective-permute-start(bf16[64,256]{0,1:T(8,128)(2,1)S(1)} %get-tuple-element.10), channel_id=1, source_target_pairs={{4,0},{8,4},{12,8},{16,12},{20,16},{24,20},{28,24},{0,28},{5,1},{9... | collective-permute-start | bytes 98312 | tf_op jit(solution)/shard_map/ppermute | solution.py:18
  13.2 0.7 compare_and_fusion
  13.9 0.7 compare_select_fusion.2
  14.7 0.7 copy.34
  15.4 0.9 copy.29
  16.4 4.6 %copy.36 = bf16[8,4,8,8192]{3,2,0,1:T(8,128)(2,1)} copy(bf16[8,4,8,8192]{3,2,1,0:T(8,128)(2,1)} %bitcast.95) | data formatting | bytes 8388608 | tf_op jit(solution)/shard_map/all_to_all | solution.py:82
  21.0 0.0 collective-permute-done
  21.0 0.0 collective-permute-done.1
  21.0 0.2 pad_maximum_fusion
  21.2 0.0 copy-start
  21.3 0.0 copy-start.1
  21.3 12.1 %gather_fusion = bf16[4096,64]{1,0:T(8,128)(2,1)S(1)} fusion(bf16[64,4608]{0,1:T(8,128)(2,1)S(1)} %pad_maximum_fusion, s32[4096]{0:T(1024)S(1)} %broadcast_clamp_fusion), kind=kCustom, calls=%fused_computation | custom fusion | bytes 1064960 | tf_op jit(solution)/shard_map/jit(_take)/gather | solution.py:76
  33.4 0.3 copy.27
  33.7 0.8 broadcast_select_fusion
  34.6 3.5 %all-to-all-start.1 = ((bf16[64,4,1024]{2,0,1:T(8,128)(2,1)}), bf16[64,4,1024]{2,0,1:T(8,128)(2,1)S(1)}, u32[]{:S(2)}, u32[]{:S(2)}) async-start(bf16[64,4,1024]{2,0,1:T(8,128)(2,1)} %broadcast_select_fusion), calls=%async_computation.1 | async-start | bytes 1048576 | tf_op jit(solution)/shard_map/all_to_all | solution.py:79
  38.1 0.0 collective-permute-done.2
  38.1 0.0 collective-permute-done.3
  38.1 0.0 copy-done
  38.1 0.0 copy-done.1
  38.1 0.7 copy.28
  38.9 4.0 %gather_fusion.1 = f32[1024,2]{1,0:T(8,128)} fusion(f32[2,4608]{0,1:T(8,128)S(1)} %copy.28, s32[1024]{0:T(1024)S(1)} %broadcast_clamp_fusion.1), kind=kCustom, calls=%fused_computation.1 | custom fusion | bytes 20480 | tf_op jit(solution)/shard_map/jit(_take)/gather | solution.py:81
  42.9 1.2 select_bitcast_fusion
  44.2 2.7 %all-to-all-done.1 = bf16[64,4,1024]{2,0,1:T(8,128)(2,1)S(1)} async-done(((bf16[64,4,1024]{2,0,1:T(8,128)(2,1)}), bf16[64,4,1024]{2,0,1:T(8,128)(2,1)S(1)}, u32[]{:S(2)}, u32[]{:S(2)}) %all-to-all-start.1) | async-done | bytes 524320 | tf_op jit(solution)/shard_map/all_to_all | solution.py:79
  46.8 5.0 %all-to-all-start = ((bf16[64,4,8192]{2,0,1:T(8,128)(2,1)}), bf16[64,4,8192]{2,0,1:T(8,128)(2,1)}, u32[]{:S(2)}, u32[]{:S(2)}) async-start(bf16[64,4,8192]{2,0,1:T(8,128)(2,1)} %bitcast.92), calls=%async_computation | async-start | bytes 8388608 | tf_op jit(solution)/shard_map/all_to_all | solution.py:82
  51.9 0.1 convert_reduce_fusion.1
  52.0 0.2 copy.30
  52.2 0.6 fusion.11
  52.8 0.1 fusion.9
  52.9 1.0 multiply_reduce_fusion
  54.6 0.3 fusion.7
  54.9 0.4 fusion.15
  55.3 0.3 fusion.12
  55.6 0.4 fusion.6
  56.0 0.4 fusion.19
  56.4 0.4 fusion.18
  56.8 0.4 fusion.5
  57.2 0.4 fusion.21
  57.5 0.4 fusion.20
  57.9 0.4 fusion.4
  58.3 0.4 fusion.23
  58.7 0.4 fusion.22
  59.1 0.4 fusion.3
  59.5 0.4 fusion.24
  59.9 0.4 fusion.25
  60.3 0.4 fusion.2
  60.6 0.4 convolution_divide_fusion
  61.0 0.1 fusion.8
  61.2 0.9 convolution_bitcast_fusion
  62.1 0.3 convolution_bitcast_fusion.1
  62.4 0.3 fusion.26
  62.7 37.2 %all-to-all-done = bf16[64,4,8192]{2,0,1:T(8,128)(2,1)} async-done(((bf16[64,4,8192]{2,0,1:T(8,128)(2,1)}), bf16[64,4,8192]{2,0,1:T(8,128)(2,1)}, u32[]{:S(2)}, u32[]{:S(2)}) %all-to-all-start) | async-done | bytes 4194336 | tf_op jit(solution)/shard_map/all_to_all | solution.py:82
  99.9 2.9 %convert_reduce_fusion = f32[8192]{0:T(1024)S(1)} fusion(bf16[64,4,8192]{2,0,1:T(8,128)(2,1)} %all-to-all-done), kind=kLoop, calls=%fused_computation.7 | loop fusion | flops 4186112 | bytes 4227072 | tf_op jit(solution)/shard_map/reduce_sum | solution.py:61
  102.8 3.3 %fusion.1 = bf16[256,8192]{1,0:T(8,128)(2,1)S(1)} fusion(f32[8192]{0:T(1024)S(1)} %broadcast_multiply_fusion, bf16[64,4,8192]{2,0,1:T(8,128)(2,1)} %all-to-all-done), kind=kLoop, calls=%fused_computation.5 | loop fusion | flops 6291456 | bytes 8421376 | tf_op jit(solution)/shard_map/convert_element_type | solution.py:62
  106.2 1.4 fusion
  107.5 50.7 %all_to_all.41 = bf16[4,64,8192]{2,1,0:T(8,128)(2,1)S(1)} all-to-all(bf16[4,64,8192]{2,1,0:T(8,128)(2,1)S(1)} %bitcast.91), channel_id=1, replica_groups=mesh['wide'=8,'narrow'=4] {'narrow'}, dimensions={0} | all-to-all | bytes 8388608 | tf_op jit(solution)/shard_map/all_to_all | solution.py:84
  158.2 2.3 %copy.33 = bf16[4,8,8,8192]{3,2,0,1:T(8,128)(2,1)} copy(bf16[4,8,8,8192]{3,2,1,0:T(8,128)(2,1)S(1)} %bitcast.93) | data formatting | bytes 8388608 | tf_op jit(solution)/shard_map/all_to_all | solution.py:84
  (8 shorter events, 0.1 us)
Async XLA Ops:
  0.7 37.3 %collective-permute-start.2 = (f32[2,256]{1,0:T(2,128)S(1)}, f32[2,256]{1,0:T(2,128)S(1)}, u32[]{:S(2)}, u32[]{:S(2)}) collective-permute-start(f32[2,256]{1,0:T(2,128)S(1)} %get-tuple-element.11), channel_id=1, source_target_pairs={{0,4},{4,8},{8,12},{12,16},{16,20},{20,24},{24,28},{28,0},{1,5},{5... | collective-permute-start | bytes 6152 | tf_op jit(solution)/shard_map/ppermute | solution.py:17
  3.7 34.3 %collective-permute-start.3 = (f32[2,256]{1,0:T(2,128)S(1)}, f32[2,256]{1,0:T(2,128)S(1)}, u32[]{:S(2)}, u32[]{:S(2)}) collective-permute-start(f32[2,256]{1,0:T(2,128)S(1)} %get-tuple-element.12), channel_id=1, source_target_pairs={{4,0},{8,4},{12,8},{16,12},{20,16},{24,20},{28,24},{0,28},{5,1},{9... | collective-permute-start | bytes 6152 | tf_op jit(solution)/shard_map/ppermute | solution.py:18
  8.4 12.6 %collective-permute-start = (bf16[64,256]{0,1:T(8,128)(2,1)S(1)}, bf16[64,256]{0,1:T(8,128)(2,1)S(1)}, u32[]{:S(2)}, u32[]{:S(2)}) collective-permute-start(bf16[64,256]{0,1:T(8,128)(2,1)S(1)} %get-tuple-element.9), channel_id=1, source_target_pairs={{0,4},{4,8},{8,12},{12,16},{16,20},{20,24},{24,28},{28,0},{1,5},{5... | collective-permute-start | bytes 98312 | tf_op jit(solution)/shard_map/ppermute | solution.py:17
  8.5 12.5 %collective-permute-start.1 = (bf16[64,256]{0,1:T(8,128)(2,1)S(1)}, bf16[64,256]{0,1:T(8,128)(2,1)S(1)}, u32[]{:S(2)}, u32[]{:S(2)}) collective-permute-start(bf16[64,256]{0,1:T(8,128)(2,1)S(1)} %get-tuple-element.10), channel_id=1, source_target_pairs={{4,0},{8,4},{12,8},{16,12},{20,16},{24,20},{28,24},{0,28},{5,1},{9... | collective-permute-start | bytes 98312 | tf_op jit(solution)/shard_map/ppermute | solution.py:18
  21.2 16.8 %copy-start = (f32[4096]{0:T(1024)S(1)}, f32[4096]{0:T(1024)}, u32[]{:S(2)}) copy-start(f32[4096]{0:T(1024)} %param.9) | copy-start | bytes 49156
  21.3 16.8 %copy-start.1 = (f32[4096]{0:T(1024)S(1)}, f32[4096]{0:T(1024)}, u32[]{:S(2)}) copy-start(f32[4096]{0:T(1024)} %param.8) | copy-start | bytes 49156
  34.6 12.3 %all-to-all-start.1 = ((bf16[64,4,1024]{2,0,1:T(8,128)(2,1)}), bf16[64,4,1024]{2,0,1:T(8,128)(2,1)S(1)}, u32[]{:S(2)}, u32[]{:S(2)}) async-start(bf16[64,4,1024]{2,0,1:T(8,128)(2,1)} %broadcast_select_fusion), calls=%async_computation.1 | async-start | bytes 1048576 | tf_op jit(solution)/shard_map/all_to_all | solution.py:79
  46.8 53.1 %all-to-all-start = ((bf16[64,4,8192]{2,0,1:T(8,128)(2,1)}), bf16[64,4,8192]{2,0,1:T(8,128)(2,1)}, u32[]{:S(2)}, u32[]{:S(2)}) async-start(bf16[64,4,8192]{2,0,1:T(8,128)(2,1)} %bitcast.92), calls=%async_computation | async-start | bytes 8388608 | tf_op jit(solution)/shard_map/all_to_all | solution.py:82
where the time goes:
time: 161 us
  blocking collectives  50.7 us (31%)
  waiting for transfers between devices  39.9 us (25%)
  local copies, waits for them, and re-layouts  27.6 us (17%)
  starting transfers between devices  19.4 us (12%)
  other arithmetic  11.7 us (7%)
  matrix products  10.2 us (6%)
    all_to_all x1, blocking collectives, body(): lax.all_to_all(result, 'narrow', split_axis=0, concat_axis=1, tiled=True)  50.7 us
    all_to_all x1, waiting for transfers between devices, body(): lax.all_to_all(states, 'narrow', split_axis=1, concat_axis=0, tiled=True)  37.2 us
    gather x2, local copies, waits for them, and re-layouts, body(): jnp.take(extended, obs_pick.reshape(-1), axis=1)  12.5 us
    ppermute x2, starting transfers between devices, padded(): after = lax.ppermute(leading, axis, down)  7.81 us
    all_to_all x1, starting transfers between devices, body(): lax.all_to_all(states, 'narrow', split_axis=1, concat_axis=0, tiled=True)  5.04 us
    all_to_all x1, local copies, waits for them, and re-layouts, body(): lax.all_to_all(states, 'narrow', split_axis=1, concat_axis=0, tiled=True)  4.64 us
    gather x1, local copies, waits for them, and re-layouts, body(): stat_rows = jnp.take(stat_pair, own_rows, axis=1)  4.04 us
    all_to_all x1, starting transfers between devices, body(): lax.all_to_all(chosen, 'narrow', split_axis=1, concat_axis=0, tiled=True)  3.47 us
  transfers between devices with their start and end apart: 6, of which 2 were waited for; matrix products, arithmetic and copies ran while one was open for 24% of the time, Pallas kernels for 0%

commit v1 on v0

--- a/solution.py
+++ b/solution.py
@@ -5,6 +5,17 @@
 
 HALO = 256
 ITERS = 6
+
+
+def _extend_loops(sheet, array_axis, mat):
+    near, seen_now = (sheet.shape[:array_axis], sheet.shape[array_axis + 1 :])
+    return jnp.moveaxis(sheet.reshape(*near, mat, -1, *seen_now), array_axis, 0)
+
+
+def spread_samples(xin, which_dim):
+    xin = jnp.moveaxis(xin, 0, which_dim)
+    w1 = xin.shape
+    return xin.reshape(*w1[:which_dim], w1[which_dim] * w1[which_dim + 1], *w1[which_dim + 2 :])
 
 
 def padded(array, sides, width):
@@ -79,7 +90,18 @@
     arrived = lax.all_to_all(chosen, "narrow", split_axis=1, concat_axis=0, tiled=True)
     picked = arrived.reshape(members, -1)
     stat_rows = jnp.take(stat_pair, own_rows, axis=1)
-    regional = lax.all_to_all(states, "narrow", split_axis=1, concat_axis=0, tiled=True)
+    shaped, top = (lax.axis_size("narrow"), lax.axis_index("narrow"))
+    block_now = _extend_loops(states, 1, shaped)
+    crops = [block_now[top]]
+    for q in tuple(range(1, shaped)):
+        z1 = block_now[(top + q) % shaped]
+        crops.append(
+            lax.ppermute(
+                z1, axis_name="narrow", perm=[(dev, (dev + q) % shaped) for dev in range(shaped)]
+            )
+        )
+    block_now = jnp.stack(crops, 0)[(top - jnp.arange(shaped)) % shaped]
+    regional = spread_samples(block_now, 0)
     result = analyse(picked.astype(jnp.float32), stat_rows[0], stat_rows[1], taper[0], regional)
     return lax.all_to_all(result, "narrow", split_axis=0, concat_axis=1, tiled=True)
 

time: 161 us -> 158 us (0.981)
  local copies, waits for them, and re-layouts: 27.6 us -> 58.9 us
  waiting for transfers between devices: 39.9 us -> 9 us
  starting transfers between devices: 19.4 us -> 16.2 us
    all_to_all x1 -> x0, waiting for transfers between devices: 37.2 us -> none  [body(): lax.all_to_all(states, 'narrow', split_axis=1, concat_axis=0, tiled=True)]
    another operation x0 -> x1, local copies, waits for them, and re-layouts: none -> 15 us
    unnamed x7 -> x21, local copies, waits for them, and re-layouts: 3.17 us -> 11.5 us
    reshape x0 -> x1, local copies, waits for them, and re-layouts: none -> 7.83 us  [_extend_loops(): return jnp.moveaxis(sheet.reshape(*near, mat, -1, *seen_now), array_axis, 0)]
    all_to_all x1, waiting for transfers between devices: 2.69 us -> 8.93 us  [body(): lax.all_to_all(chosen, 'narrow', split_axis=1, concat_axis=0, tiled=True)]
    all_to_all x1 -> x0, starting transfers between devices: 5.04 us -> none  [body(): lax.all_to_all(states, 'narrow', split_axis=1, concat_axis=0, tiled=True)]
    gather x0 -> x1, local copies, waits for them, and re-layouts: none -> 4.94 us  [body(): block_now = jnp.stack(crops, 0)[(top - jnp.arange(shaped)) % shaped]]
    all_to_all x1 -> x0, local copies, waits for them, and re-layouts: 4.64 us -> none  [body(): lax.all_to_all(states, 'narrow', split_axis=1, concat_axis=0, tiled=True)]
  transfers between devices with their start and end apart: 6 -> 8, of which waited for: 2 -> 2; matrix products, arithmetic and copies ran while one was open for 24% -> 24% of each run, Pallas kernels for 0% -> 0%
where the time goes in v1:
time: 158 us
  local copies, waits for them, and re-layouts  58.9 us (37%)
  blocking collectives  51.5 us (33%)
  starting transfers between devices  16.2 us (10%)
  other arithmetic  11 us (7%)
  matrix products  10.1 us (6%)
  waiting for transfers between devices  9 us (6%)
    all_to_all x1, blocking collectives, body(): lax.all_to_all(result, 'narrow', split_axis=0, concat_axis=1, tiled=True)  51.5 us
    another operation x1, local copies, waits for them, and re-layouts  15 us
    gather x2, local copies, waits for them, and re-layouts, body(): jnp.take(extended, obs_pick.reshape(-1), axis=1)  12.5 us
    unnamed x21, local copies, waits for them, and re-layouts  11.5 us
    ppermute x2, starting transfers between devices, padded(): after = lax.ppermute(leading, axis, down)  9.3 us
    all_to_all x1, waiting for transfers between devices, body(): lax.all_to_all(chosen, 'narrow', split_axis=1, concat_axis=0, tiled=True)  8.93 us
    reshape x1, local copies, waits for them, and re-layouts, _extend_loops(): return jnp.moveaxis(sheet.reshape(*near, mat, -1, *seen_now), array_axis, 0)  7.83 us
    gather x1, local copies, waits for them, and re-layouts, body(): block_now = jnp.stack(crops, 0)[(top - jnp.arange(shaped)) % shaped]  4.94 us
  transfers between devices with their start and end apart: 8, of which 2 were waited for; matrix products, arithmetic and copies ran while one was open for 24% of the time, Pallas kernels for 0%

profile of v1, /device:TPU:0, one launch (start us, length us, event | category | flops | bytes accessed | tf_op | source)
XLA Modules:
  0.0 157.8 jit_solution(15635196586319729200)
XLA Ops:
  0.0 7.8 %reshape.193 = bf16[64,4,8192]{2,1,0:T(4,128)(2,1)} reshape(bf16[64,32768]{1,0:T(8,128)(2,1)} %param.6) | data formatting | bytes 8388608 | tf_op jit(solution)/shard_map/reshape | solution.py:12
  7.8 15.0 %constant_dynamic-slice_fusion.4 = (bf16[64,1,8192]{2,1,0:T(2,128)(2,1)S(1)}, bf16[64,1,8192]{2,1,0:T(2,128)(2,1)S(1)}, bf16[64,1,8192]{2,1,0:T(2,128)(2,1)S(1)}, bf16[64,1,8192]{2,1,0:T(2,128)(2,1)S(1)}) fusion(bf16[64,4,8192]{2,1,0:T(4,128)(2,1)} %reshape.193, s32[]{:T(128)S(6)} %select_n.94, s32[]{:T(128)S(6)} %select_n.100, s32[]{:T(128)S(6)} %select_n.98, ...), kind=kLoop, calls=%fused_computation.72 | loop fusion | bytes 8388624 | tf_op jit(solution)/shard_map/dynamic-slice
  22.8 2.1 %copy.48 = bf16[64,1,8192]{2,0,1:T(8,128)(2,1)} copy(bf16[64,1,8192]{2,1,0:T(2,128)(2,1)S(1)} %get-tuple-element.10) | data formatting | bytes 2097152
  24.9 2.4 %collective-permute-start.2 = (bf16[64,8192]{1,0:T(8,128)(2,1)}, bf16[64,8192]{1,0:T(8,128)(2,1)}, u32[]{:S(2)}, u32[]{:S(2)}) collective-permute-start(bf16[64,8192]{1,0:T(8,128)(2,1)} %bitcast.98), channel_id=1, source_target_pairs={{0,3},{1,0},{2,1},{3,2},{4,7},{5,4},{6,5},{7,6},{8,11},{9,8},{10,9... | collective-permute-start | bytes 3145736 | tf_op jit(solution)/shard_map/ppermute | solution.py:99
  27.4 2.1 %copy.49 = bf16[64,1,8192]{2,0,1:T(8,128)(2,1)} copy(bf16[64,1,8192]{2,1,0:T(2,128)(2,1)S(1)} %get-tuple-element.11) | data formatting | bytes 2097152
  29.5 0.6 collective-permute-start.1
  30.0 2.1 %copy.50 = bf16[64,1,8192]{2,0,1:T(8,128)(2,1)} copy(bf16[64,1,8192]{2,1,0:T(2,128)(2,1)S(1)} %get-tuple-element.12) | data formatting | bytes 2097152
  32.2 0.2 collective-permute-start
  32.4 1.5 copy.30
  33.9 4.6 %collective-permute-start.4 = (bf16[64,256]{0,1:T(8,128)(2,1)S(1)}, bf16[64,256]{0,1:T(8,128)(2,1)S(1)}, u32[]{:S(2)}, u32[]{:S(2)}) collective-permute-start(bf16[64,256]{0,1:T(8,128)(2,1)S(1)} %get-tuple-element.14), channel_id=1, source_target_pairs={{4,0},{8,4},{12,8},{16,12},{20,16},{24,20},{28,24},{0,28},{5,1},{9... | collective-permute-start | bytes 98312 | tf_op jit(solution)/shard_map/ppermute | solution.py:29
  38.5 0.0 collective-permute-start.3
  38.7 2.1 %copy.51 = bf16[64,1,8192]{2,0,1:T(8,128)(2,1)} copy(bf16[64,1,8192]{2,1,0:T(2,128)(2,1)S(1)} %get-tuple-element.9) | data formatting | bytes 2097152
  40.9 1.0 copy.35
  41.9 0.0 collective-permute-done.4
  41.9 4.7 %collective-permute-start.6 = (f32[2,256]{1,0:T(2,128)S(1)}, f32[2,256]{1,0:T(2,128)S(1)}, u32[]{:S(2)}, u32[]{:S(2)}) collective-permute-start(f32[2,256]{1,0:T(2,128)S(1)} %get-tuple-element.16), channel_id=1, source_target_pairs={{4,0},{8,4},{12,8},{16,12},{20,16},{24,20},{28,24},{0,28},{5,1},{9... | collective-permute-start | bytes 6152 | tf_op jit(solution)/shard_map/ppermute | solution.py:29
  46.6 0.0 collective-permute-done.3
  46.6 0.0 collective-permute-start.5
  46.6 0.2 pad_maximum_fusion.1
  46.9 12.1 %gather_fusion.1 = bf16[4096,64]{1,0:T(8,128)(2,1)S(1)} fusion(bf16[64,4608]{0,1:T(8,128)(2,1)S(1)} %pad_maximum_fusion.1, s32[4096]{0:T(1024)S(1)} %broadcast_clamp_fusion), kind=kCustom, calls=%fused_computation.1 | custom fusion | bytes 1064960 | tf_op jit(solution)/shard_map/jit(_take)/gather | solution.py:87
  59.0 0.3 copy.33
  59.4 0.9 broadcast_select_fusion
  60.2 3.6 %all-to-all-start = ((bf16[64,4,1024]{2,0,1:T(8,128)(2,1)}), bf16[64,4,1024]{2,0,1:T(8,128)(2,1)S(1)}, u32[]{:S(2)}, u32[]{:S(2)}) async-start(bf16[64,4,1024]{2,0,1:T(8,128)(2,1)} %broadcast_select_fusion), calls=%async_computation | async-start | bytes 1048576 | tf_op jit(solution)/shard_map/all_to_all | solution.py:90
  63.9 0.0 collective-permute-done.6
  63.9 0.0 collective-permute-done.5
  63.9 0.7 copy.34
  64.7 4.0 %gather_fusion.2 = f32[1024,2]{1,0:T(8,128)} fusion(f32[2,4608]{0,1:T(8,128)S(1)} %copy.34, s32[1024]{0:T(1024)S(1)} %broadcast_clamp_fusion.1), kind=kCustom, calls=%fused_computation.2 | custom fusion | bytes 20480 | tf_op jit(solution)/shard_map/jit(_take)/gather | solution.py:92
  68.6 1.2 select_bitcast_fusion
  69.9 8.9 %all-to-all-done = bf16[64,4,1024]{2,0,1:T(8,128)(2,1)S(1)} async-done(((bf16[64,4,1024]{2,0,1:T(8,128)(2,1)}), bf16[64,4,1024]{2,0,1:T(8,128)(2,1)S(1)}, u32[]{:S(2)}, u32[]{:S(2)}) %all-to-all-start) | async-done | bytes 524320 | tf_op jit(solution)/shard_map/all_to_all | solution.py:90
  78.8 0.1 convert_reduce_fusion.1
  78.9 0.2 copy.36
  79.2 0.6 fusion.11
  79.7 0.1 fusion.9
  79.9 0.9 multiply_reduce_fusion
  81.4 0.3 fusion.7
  81.7 0.3 fusion.12
  82.0 0.4 fusion.15
  82.4 0.4 fusion.6
  82.8 0.4 fusion.20
  83.1 0.4 fusion.21
  83.5 0.4 fusion.5
  83.9 0.4 fusion.22
  84.3 0.4 fusion.23
  84.7 0.4 fusion.4
  85.1 0.4 fusion.24
  85.5 0.4 fusion.25
  85.9 0.4 fusion.3
  86.3 0.4 fusion.26
  86.6 0.4 fusion.27
  87.1 0.4 fusion.2
  87.5 0.4 convolution_divide_fusion
  87.8 0.1 fusion.8
  88.0 0.9 convolution_bitcast_fusion
  88.9 0.3 convolution_bitcast_fusion.1
  89.2 0.3 fusion.28
  89.5 0.1 collective-permute-done.1
  89.6 0.0 collective-permute-done
  89.6 3.6 %pad_maximum_fusion = bf16[4,64,8192]{2,1,0:T(8,128)(2,1)} fusion(bf16[1,64,8192]{2,1,0:T(8,128)(2,1)} %bitcast.2, bf16[1,64,8192]{2,1,0:T(8,128)(2,1)} %bitcast.1, bf16[1,64,8192]{2,1,0:T(8,128)(2,1)} %bitcast, bf16[1,64,8192]{2,1,0:T(8,128)(2,1)S(1)} %bitcast.105), kind=kLoop, calls=%fused_computation.7 | loop fusion | flops 6291456 | bytes 8388608 | tf_op jit(solution)/shard_map/stack | solution.py:103
  93.2 4.9 %gather_fusion = bf16[4,64,8192]{2,1,0:T(8,128)(2,1)} fusion(bf16[4,64,8192]{2,1,0:T(8,128)(2,1)} %pad_maximum_fusion, s32[1024]{0:T(1024)S(1)} %pad_clamp_fusion), kind=kCustom, calls=%fused_computation | custom fusion | bytes 8388624 | tf_op jit(solution)/shard_map/gather | solution.py:103
  98.2 3.0 %convert_reduce_fusion = f32[8192]{0:T(1024)S(1)} fusion(bf16[4,64,8192]{2,1,0:T(8,128)(2,1)} %gather_fusion), kind=kLoop, calls=%fused_computation.8 | loop fusion | flops 4186112 | bytes 4227072 | tf_op jit(solution)/shard_map/reduce_sum | solution.py:72
  101.2 0.4 copy-done
  101.6 0.9 fusion.1
  102.6 1.4 fusion
  104.0 51.5 %all_to_all.28 = bf16[4,64,8192]{2,1,0:T(8,128)(2,1)S(1)} all-to-all(bf16[4,64,8192]{2,1,0:T(8,128)(2,1)S(1)} %bitcast.102), channel_id=1, replica_groups=mesh['wide'=8,'narrow'=4] {'narrow'}, dimensions={0} | all-to-all | bytes 8388608 | tf_op jit(solution)/shard_map/all_to_all | solution.py:106
  155.5 2.3 %copy.42 = bf16[4,8,8,8192]{3,2,0,1:T(8,128)(2,1)} copy(bf16[4,8,8,8192]{3,2,1,0:T(8,128)(2,1)S(1)} %bitcast.103) | data formatting | bytes 8388608 | tf_op jit(solution)/shard_map/all_to_all | solution.py:106
  (28 shorter events, 0.2 us)
Async XLA Ops:
  24.9 13.6 %copy-start.3 = (s32[4,1024]{1,0:T(4,128)S(1)}, s32[4,1024]{1,0:T(4,128)}, u32[]{:S(2)}) copy-start(s32[4,1024]{1,0:T(4,128)} %param.10) | copy-start | bytes 49156
  24.9 13.8 %copy-start.4 = (f32[4096]{0:T(1024)S(1)}, f32[4096]{0:T(1024)}, u32[]{:S(2)}) copy-start(f32[4096]{0:T(1024)} %param.9) | copy-start | bytes 49156
  24.9 13.8 %copy-start.5 = (f32[4096]{0:T(1024)S(1)}, f32[4096]{0:T(1024)}, u32[]{:S(2)}) copy-start(f32[4096]{0:T(1024)} %param.8) | copy-start | bytes 49156
  24.9 64.6 %collective-permute-start.2 = (bf16[64,8192]{1,0:T(8,128)(2,1)}, bf16[64,8192]{1,0:T(8,128)(2,1)}, u32[]{:S(2)}, u32[]{:S(2)}) collective-permute-start(bf16[64,8192]{1,0:T(8,128)(2,1)} %bitcast.98), channel_id=1, source_target_pairs={{0,3},{1,0},{2,1},{3,2},{4,7},{5,4},{6,5},{7,6},{8,11},{9,8},{10,9... | collective-permute-start | bytes 3145736 | tf_op jit(solution)/shard_map/ppermute | solution.py:99
  29.5 11.4 %copy-start.6 = (f32[1,1024]{1,0:T(1,128)S(1)}, f32[1,1024]{1,0:T(1,128)}, u32[]{:S(2)}) copy-start(f32[1,1024]{1,0:T(1,128)} %param.11) | copy-start | bytes 12292
  29.5 60.1 %collective-permute-start.1 = (bf16[64,8192]{1,0:T(8,128)(2,1)}, bf16[64,8192]{1,0:T(8,128)(2,1)}, u32[]{:S(2)}, u32[]{:S(2)}) collective-permute-start(bf16[64,8192]{1,0:T(8,128)(2,1)} %bitcast.99), channel_id=1, source_target_pairs={{0,2},{1,3},{2,0},{3,1},{4,6},{5,7},{6,4},{7,5},{8,10},{9,11},{10,... | collective-permute-start | bytes 3145736 | tf_op jit(solution)/shard_map/ppermute | solution.py:99
  32.2 57.4 %collective-permute-start = (bf16[64,8192]{1,0:T(8,128)(2,1)}, bf16[64,8192]{1,0:T(8,128)(2,1)}, u32[]{:S(2)}, u32[]{:S(2)}) collective-permute-start(bf16[64,8192]{1,0:T(8,128)(2,1)} %bitcast.100), channel_id=1, source_target_pairs={{0,1},{1,2},{2,3},{3,0},{4,5},{5,6},{6,7},{7,4},{8,9},{9,10},{10,1... | collective-permute-start | bytes 3145736 | tf_op jit(solution)/shard_map/ppermute | solution.py:99
  33.9 8.0 %collective-permute-start.4 = (bf16[64,256]{0,1:T(8,128)(2,1)S(1)}, bf16[64,256]{0,1:T(8,128)(2,1)S(1)}, u32[]{:S(2)}, u32[]{:S(2)}) collective-permute-start(bf16[64,256]{0,1:T(8,128)(2,1)S(1)} %get-tuple-element.14), channel_id=1, source_target_pairs={{4,0},{8,4},{12,8},{16,12},{20,16},{24,20},{28,24},{0,28},{5,1},{9... | collective-permute-start | bytes 98312 | tf_op jit(solution)/shard_map/ppermute | solution.py:29
  38.5 8.1 %collective-permute-start.3 = (bf16[64,256]{0,1:T(8,128)(2,1)S(1)}, bf16[64,256]{0,1:T(8,128)(2,1)S(1)}, u32[]{:S(2)}, u32[]{:S(2)}) collective-permute-start(bf16[64,256]{0,1:T(8,128)(2,1)S(1)} %get-tuple-element.13), channel_id=1, source_target_pairs={{0,4},{4,8},{8,12},{12,16},{16,20},{20,24},{24,28},{28,0},{1,5},{5... | collective-permute-start | bytes 98312 | tf_op jit(solution)/shard_map/ppermute | solution.py:28
  41.9 22.0 %collective-permute-start.6 = (f32[2,256]{1,0:T(2,128)S(1)}, f32[2,256]{1,0:T(2,128)S(1)}, u32[]{:S(2)}, u32[]{:S(2)}) collective-permute-start(f32[2,256]{1,0:T(2,128)S(1)} %get-tuple-element.16), channel_id=1, source_target_pairs={{4,0},{8,4},{12,8},{16,12},{20,16},{24,20},{28,24},{0,28},{5,1},{9... | collective-permute-start | bytes 6152 | tf_op jit(solution)/shard_map/ppermute | solution.py:29
  46.6 17.3 %collective-permute-start.5 = (f32[2,256]{1,0:T(2,128)S(1)}, f32[2,256]{1,0:T(2,128)S(1)}, u32[]{:S(2)}, u32[]{:S(2)}) collective-permute-start(f32[2,256]{1,0:T(2,128)S(1)} %get-tuple-element.15), channel_id=1, source_target_pairs={{0,4},{4,8},{8,12},{12,16},{16,20},{20,24},{24,28},{28,0},{1,5},{5... | collective-permute-start | bytes 6152 | tf_op jit(solution)/shard_map/ppermute | solution.py:28
  59.0 20.1 %copy-start.2 = (f32[1,1024]{0,1:T(8,128)S(1)}, f32[1,1024]{0,1:T(8,128)}, u32[]{:S(2)}) copy-start(f32[1,1024]{0,1:T(8,128)} %copy.35) | copy-start | bytes 12292
  60.2 18.6 %all-to-all-start = ((bf16[64,4,1024]{2,0,1:T(8,128)(2,1)}), bf16[64,4,1024]{2,0,1:T(8,128)(2,1)S(1)}, u32[]{:S(2)}, u32[]{:S(2)}) async-start(bf16[64,4,1024]{2,0,1:T(8,128)(2,1)} %broadcast_select_fusion), calls=%async_computation | async-start | bytes 1048576 | tf_op jit(solution)/shard_map/all_to_all | solution.py:90
  85.5 4.1 %copy-start.1 = (bf16[64,1,8192]{2,0,1:T(8,128)(2,1)S(1)}, bf16[64,1,8192]{2,0,1:T(8,128)(2,1)}, u32[]{:S(2)}) copy-start(bf16[64,1,8192]{2,0,1:T(8,128)(2,1)} %copy.51) | copy-start | bytes 3145732
  98.2 3.4 %copy-start = (bf16[4,64,8192]{2,1,0:T(8,128)(2,1)S(1)}, bf16[4,64,8192]{2,1,0:T(8,128)(2,1)}, u32[]{:S(2)}) copy-start(bf16[4,64,8192]{2,1,0:T(8,128)(2,1)} %gather_fusion) | copy-start | bytes 12582916
